TPU v7x, 128 devices: a whole 4x4x4 slice. The times are simulated.
128 devices in a mesh: dp: 8 (over z, core), seq: 16 (over x, y).
Axes of the slice: x: 4, y: 4, z: 4, core: 2. Of those that a mesh axis runs over, the one named last changes fastest.
Arguments:
- queries: bfloat16 [16384, 4096], P(('dp', 'seq')), may hold values from -6 to 6
- keys: bfloat16 [16384, 512], P(('dp', 'seq')), may hold values from -6 to 6
- values: bfloat16 [16384, 512], P(('dp', 'seq')), may hold values from -6 to 6
- grad_out: bfloat16 [16384, 4096], P(('dp', 'seq')), may hold values from -6 to 6
- doc_lengths: int32 [32], replicated, may hold values from 1 to 2048, 16384 in all
Outputs:
- grad_q: bfloat16 [16384, 4096], P(('dp', 'seq'))
- grad_k: bfloat16 [16384, 512], P(('dp', 'seq'))
- grad_v: bfloat16 [16384, 512], P(('dp', 'seq'))
Inputs may be any that keep to these rules, and one draw needn't show every extreme that they name: `doc_lengths`: the 32 lengths sum to 16384; the longest is exactly 2048.
All inputs are finite; a program needn't handle non-finite values.
Results may differ from a plain program's by a relative error of at most 0.0071.
Values may be sent and summed in bfloat16 or wider, within the bound.
A program may use at most 64 MiB of HBM per device.

v0:
```python
import functools

import jax
import jax.numpy as jnp
from jax import lax
from jax.experimental import pallas as pl
from jax.experimental.pallas import tpu as pltpu
from jax.sharding import PartitionSpec as P

MESH = pl.DeviceIdType.MESH
SIDE = 4
TOK = 128
HD = 128
GW = 1024
PER_KV = GW // HD
GROUP = SIDE * SIDE * TOK
WIN = 2 * GROUP
KB = 256
SLOTS = 24
EARLIEST = (0, 3, 8, 15)
FROM_X = (0, 1, 3, 2)
LOG2E = 1.4426950408889634
INV_ROOT = HD ** -0.5
LOW = -1e30
SCALE2 = INV_ROOT * LOG2E


def place():
    seq = lax.axis_index("seq")
    return lax.axis_index("dp"), lax.div(seq, SIDE), lax.rem(seq, SIDE)


def greet(dp, x, y):
    barrier = pltpu.get_barrier_semaphore()
    count = lax.axis_size("dp")
    peers = [{"seq": lax.rem(x + d, SIDE) * SIDE + y} for d in range(1, SIDE)]
    peers += [{"seq": x * SIDE + lax.rem(y + d, SIDE)} for d in range(1, SIDE)]
    peers += [{"dp": lax.rem(dp + 1, count)}, {"dp": lax.rem(dp + count - 1, count)}]
    for peer in peers:
        pl.semaphore_signal(barrier, inc=1, device_id=peer, device_id_type=MESH)
    pl.semaphore_wait(barrier, len(peers))


def cols(index, width):
    return pl.ds(pl.multiple_of(index * width, width), width)


def fold(tile):
    return tile.reshape(KB // 8, 8, HD)


def step_kernel(
    q, o, k, v, lens, out_q, out_k, out_v,
    land, kv, qs, os, s_buf, dp_buf, stats, run, final, dq, lows,
    gq, z_out, z_in, own, y_out, y_in, x_out, send, recv, here,
):
    dp, x, y = place()
    count = lax.axis_size("dp")
    used = [0]

    def remote(src, dst, device):
        i = used[0]
        used[0] += 1
        copy = pltpu.make_async_remote_copy(
            src_ref=src, dst_ref=dst, send_sem=send.at[i], recv_sem=recv.at[i],
            device_id=device, device_id_type=MESH,
        )
        copy.start()
        return copy

    def local_copy(src, dst, i):
        copy = pltpu.make_async_copy(src, dst, here.at[i])
        copy.start()
        return copy

    def at_x(d):
        return {"seq": lax.rem(x + d, SIDE) * SIDE + y}

    def at_y(d):
        return {"seq": x * SIDE + lax.rem(y + d, SIDE)}

    after = {"dp": lax.rem(dp + 1, count)}
    before = {"dp": lax.rem(dp + count - 1, count)}
    heads = [slice(h * HD, (h + 1) * HD) for h in range(PER_KV)]

    kv_here = [local_copy(a.at[:, cols(x, HD)], kv.at[n, 1, x, y], n) for n, a in enumerate((k, v))]
    q_here = [local_copy(a.at[:, cols(x, GW)], land.at[0, n], 2 + n) for n, a in enumerate((q, o))]
    greet(dp, x, y)
    first = []
    for d in (1, 3, 2):
        for n, a in enumerate((k, v)):
            head = lax.rem(x + d, SIDE)
            first.append(remote(a.at[:, cols(head, HD)], kv.at[n, 1, x, y], at_x(d)))
    arrive = {}
    for d in (3, 1, 2):
        slot = FROM_X.index(SIDE - d)
        head = lax.rem(x + d, SIDE)
        arrive[slot] = [
            remote(a.at[:, cols(head, GW)], land.at[slot, n], at_x(d)) for n, a in enumerate((q, o))
        ]

    def take(slot):
        for copy in q_here if slot == 0 else arrive[slot]:
            if slot == 0:
                copy.wait()
            else:
                copy.wait_recv()
        for h, span in enumerate(heads):
            qs[slot, span, :] = land[slot, 0, :, span]
            os[slot, span, :] = land[slot, 1, :, span]

    for copy in kv_here:
        copy.wait()
    for copy in first:
        copy.wait_recv()
    mine = kv.at[:, 1, :, y]
    along = [remote(mine, mine, at_y(d)) for d in (1, 3)]
    later = [remote(mine, kv.at[:, 0, :, y], after)]
    onward = []
    for copy, d in zip(along, (1, 3)):
        copy.wait_recv()
        source = lax.rem(y + SIDE - d, SIDE)
        part = kv.at[:, 1, pl.ds(d - 1 if d == 1 else 2, 2), source]
        onward.append(remote(part, part, at_y(d)))
        later.append(remote(kv.at[:, 1, :, source], kv.at[:, 0, :, source], after))
    take(0)
    run[...] = jnp.zeros_like(run)

    def at_least(value, bound):
        return (value >= bound).astype(jnp.int32)

    first_key = (dp - 1) * GROUP
    spots, steps, bases, blocks = [], [], [], []
    ready = jnp.int32(0)
    for slot in range(SIDE):
        block = lax.rem(x + FROM_X[slot], SIDE) * SIDE + y
        head_pos = dp * GROUP + block * TOK
        pos = head_pos + lax.broadcasted_iota(jnp.int32, (8, TOK), 1)

        def one_doc(i, state):
            end, low, low_row = state
            end = end + lens[i]
            low = jnp.maximum(low, end * at_least(head_pos, end))
            low_row = jnp.where(end <= pos, end, low_row)
            return end, low, low_row

        zero = jnp.int32(0)
        _, low, low_row = lax.fori_loop(
            0, lens.shape[0], one_doc, (zero, zero, jnp.zeros((8, TOK), jnp.int32))
        )
        lows[slot] = low_row - first_key
        end_block = GROUP // TOK + block + 1
        length = lax.div(end_block - lax.div(low - first_key, TOK) + 1, 2)
        spot = jnp.maximum(ready, EARLIEST[slot])
        ready = spot + length
        spots.append(spot)
        steps.append(length)
        bases.append(jnp.maximum(0, end_block - 2 * length))
        blocks.append(block)

    def pick(slot, values):
        picked = values[0]
        for n in range(1, SIDE):
            picked = picked + at_least(slot, n) * (values[n] - values[n - 1])
        return picked

    def step_of(i):
        slot = sum(at_least(i, spot) for spot in spots[1:])
        j = i - pick(slot, spots)
        lead = pick(slot, bases) + 2 * jnp.minimum(j, pick(slot, steps) - 1)
        return slot, j, jnp.minimum(lead, WIN // TOK - 2)

    def rows(n, lead):
        pieces = []
        for c in (lead, lead + 1):
            pieces.append(kv[n, lax.shift_right_logical(c, 4), lax.shift_right_logical(c, 2) & 3, c & 3])
        return jnp.concatenate(pieces, axis=0)

    nt = (((1,), (1,)), ((), ()))
    tn = (((0,), (0,)), ((), ()))
    nn = (((1,), (0,)), ((), ()))

    def dot(a, b, dims):
        return lax.dot_general(a, b, dims, preferred_element_type=jnp.float32)

    def score_step(i):
        slot, j, lead = step_of(i)
        scores = dot(rows(0, lead), qs[slot], nt)
        dprobs = dot(rows(1, lead), os[slot], nt)
        key = lead * TOK + lax.broadcasted_iota(jnp.int32, (KB, TOK), 0)
        last = GROUP + pick(slot, blocks) * TOK + lax.broadcasted_iota(jnp.int32, (KB, TOK), 1)
        new_block = jnp.broadcast_to(j, (8, HD)) == 0
        allowed = (key >= jnp.broadcast_to(lows[slot][0:1], (KB, TOK))) & (key <= last)
        for h, span in enumerate(heads):
            tile = jnp.where(allowed, scores[:, span] * SCALE2, LOW)
            s_buf[i, :, :, span] = tile.reshape(2, TOK, HD)
            dprob = dprobs[:, span]
            dp_buf[i, :, span] = dprob.astype(jnp.bfloat16)
            old = jnp.where(new_block, LOW, run[0, :, span])
            new = jnp.maximum(old, jnp.max(fold(tile), axis=0))
            weight = jnp.exp2(fold(tile) - new[None])
            shrink = jnp.exp2(old - new)
            norm = jnp.where(new_block, 0.0, run[1, :, span])
            dots = jnp.where(new_block, 0.0, run[2, :, span])
            norm = norm * shrink + jnp.sum(weight, axis=0)
            dots = dots * shrink + jnp.sum(weight * fold(dprob), axis=0)
            for n, value in enumerate((new, norm, dots)):
                run[n, :, span] = value
                stats[i, n, :, span] = value

    for copy, d in zip(onward, (1, 3)):
        copy.wait_recv()
    far = lax.rem(y + 2, SIDE)
    later.append(remote(kv.at[:, 1, :, far], kv.at[:, 0, :, far], after))
    for copy in later:
        copy.wait_recv()
    for slot in range(SIDE):
        if slot:
            take(slot)
        pl.loop(EARLIEST[slot], (EARLIEST + (SLOTS,))[slot + 1])(score_step)

    for slot in range(SIDE):
        end = jnp.minimum(spots[slot] + steps[slot], SLOTS) - 1
        part = stats[end, 0]
        peak = jnp.max(part, axis=0, keepdims=True)
        share = jnp.exp2(part - peak)
        total = jnp.sum(stats[end, 1] * share, axis=0, keepdims=True)
        delta = jnp.sum(stats[end, 2] * share, axis=0, keepdims=True) / total
        final[slot, 0] = jnp.broadcast_to(peak + jnp.log2(total), part.shape)
        final[slot, 1] = jnp.broadcast_to(delta, part.shape)

    dq[...] = jnp.zeros_like(dq)

    @pl.loop(0, SLOTS)
    def _(i):
        slot, j, lead = step_of(i)
        probs, dscores = [], []
        for h, span in enumerate(heads):
            prob = jnp.exp2(fold(s_buf[i, :, :, span]) - final[slot, 0, :, span][None])
            dprob = fold(dp_buf[i, :, span].astype(jnp.float32))
            dscore = prob * (dprob - final[slot, 1, :, span][None])
            probs.append(prob.reshape(KB, TOK).astype(jnp.bfloat16))
            dscores.append(dscore.reshape(KB, TOK).astype(jnp.bfloat16))
        probs = jnp.concatenate(probs, axis=1)
        dscores = jnp.concatenate(dscores, axis=1)
        s_buf[i, :, :, 0:HD] = dot(dscores, qs[slot], nn).reshape(2, TOK, HD)
        s_buf[i, :, :, HD:2 * HD] = dot(probs, os[slot], nn).reshape(2, TOK, HD)
        now = dq[...] * jnp.minimum(j, 1).astype(jnp.float32) + dot(rows(0, lead), dscores, tn)
        dq[...] = now
        dp_buf[i, 0:HD, :] = (now * INV_ROOT).astype(jnp.bfloat16)

    def key_sum(c):
        sums = [jnp.zeros((TOK, HD), jnp.float32)] * 2
        for slot in range(SIDE):
            off = c - bases[slot]
            inside = (at_least(off, 0) * at_least(2 * steps[slot] - 1, off)).astype(jnp.float32)
            i = jnp.clip(spots[slot] + lax.shift_right_arithmetic(off, 1), 0, SLOTS - 1)
            for n in range(2):
                sums[n] += inside * s_buf[i, off & 1, :, n * HD:(n + 1) * HD]
        return sums[0] * INV_ROOT, sums[1]

    down = {}
    order = (2, 1, 3, 0)
    for d in order:
        column = lax.rem(y + d, SIDE)

        @pl.loop(0, SIDE)
        def _(row):
            for n, total in enumerate(key_sum(row * SIDE + column)):
                z_out[d, n, row] = total.astype(jnp.bfloat16)

        down[d] = remote(z_out.at[d], z_in.at[d], before)

    back_q = []
    for slot in (3, 1, 2, 0):
        end = jnp.minimum(spots[slot] + steps[slot], SLOTS) - 1
        for h, span in enumerate(heads):
            gq[slot, :, span] = dp_buf[end, 0:HD, span].T
        if slot:
            back_q.append(remote(gq.at[slot], out_q.at[:, cols(x, GW)], at_x(FROM_X[slot])))
    own_q = local_copy(gq.at[0], out_q.at[:, cols(x, GW)], 4)

    across = {}
    for d in order:
        column = lax.rem(y + d, SIDE)

        @pl.loop(0, SIDE)
        def _(row):
            for n, total in enumerate(key_sum(GROUP // TOK + row * SIDE + column)):
                own[d, n, row] = total

    def total(d):
        down[d].wait_recv()
        return own[d] + z_in[d].astype(jnp.float32)

    for d in order[:3]:
        y_out[d - 1] = total(d).astype(jnp.bfloat16)
        across[d] = remote(y_out.at[d - 1], y_in.at[d - 1], at_y(d))
    rest = total(0)
    for d in order[:3]:
        across[d].wait_recv()
        rest = rest + y_in[d - 1].astype(jnp.float32)
    x_out[...] = rest.astype(jnp.bfloat16)
    back = []
    for d in (2, 1, 3):
        target = lax.rem(x + d, SIDE)
        for n, out in enumerate((out_k, out_v)):
            back.append(remote(x_out.at[n, target], out.at[:, cols(x, HD)], at_x(d)))
    own_kv = [local_copy(x_out.at[n, x], out.at[:, cols(x, HD)], 5 + n) for n, out in enumerate((out_k, out_v))]
    for copy in back_q + back:
        copy.wait_recv()
    for copy in [own_q] + own_kv:
        copy.wait()
    gone = first + along + later + onward + back_q + back
    for copies in list(arrive.values()) + [list(down.values()), list(across.values()), gone]:
        for copy in copies:
            copy.wait_send()


VMEM_GRANT = 57 * 1024 * 1024
COPIES = 6 + 6 + 2 + 2 + 4 + 4 + 3 + 3 + 6


def one_step(queries, grad_out, keys, values, doc_lengths):
    piece = (2, SIDE, TOK, HD)
    wide = PER_KV * TOK
    hbm = pl.BlockSpec(memory_space=pltpu.HBM)
    arguments = [
        pltpu.with_memory_space_constraint(a, pltpu.HBM) for a in (queries, grad_out, keys, values)
    ]
    return pl.pallas_call(
        step_kernel,
        out_shape=(
            jax.ShapeDtypeStruct((TOK, SIDE * GW), jnp.bfloat16),
            jax.ShapeDtypeStruct((TOK, SIDE * HD), jnp.bfloat16),
            jax.ShapeDtypeStruct((TOK, SIDE * HD), jnp.bfloat16),
        ),
        in_specs=[hbm] * 4 + [pl.BlockSpec(memory_space=pltpu.SMEM)],
        out_specs=(pl.BlockSpec(memory_space=pl.ANY),) * 3,
        scratch_shapes=[
            pltpu.VMEM((SIDE, 2, TOK, GW), jnp.bfloat16),
            pltpu.VMEM((2, 2, SIDE, SIDE, TOK, HD), jnp.bfloat16),
            pltpu.VMEM((SIDE, wide, HD), jnp.bfloat16),
            pltpu.VMEM((SIDE, wide, HD), jnp.bfloat16),
            pltpu.VMEM((SLOTS, 2, TOK, wide), jnp.float32),
            pltpu.VMEM((SLOTS, KB, wide), jnp.bfloat16),
            pltpu.VMEM((SLOTS, 3, 8, wide), jnp.float32),
            pltpu.VMEM((3, 8, wide), jnp.float32),
            pltpu.VMEM((SIDE, 2, 8, wide), jnp.float32),
            pltpu.VMEM((HD, wide), jnp.float32),
            pltpu.VMEM((SIDE, 8, TOK), jnp.int32),
            pltpu.VMEM((SIDE, TOK, GW), jnp.bfloat16),
            pltpu.VMEM((SIDE,) + piece, jnp.bfloat16),
            pltpu.VMEM((SIDE,) + piece, jnp.bfloat16),
            pltpu.VMEM((SIDE,) + piece, jnp.float32),
            pltpu.VMEM((3,) + piece, jnp.bfloat16),
            pltpu.VMEM((3,) + piece, jnp.bfloat16),
            pltpu.VMEM(piece, jnp.bfloat16),
            pltpu.SemaphoreType.DMA((COPIES,)),
            pltpu.SemaphoreType.DMA((COPIES,)),
            pltpu.SemaphoreType.DMA((7,)),
        ],
        compiler_params=pltpu.CompilerParams(
            collective_id=0, has_side_effects=True, vmem_limit_bytes=VMEM_GRANT
        ),
        name="step",
    )(*arguments, doc_lengths)


def emit_kernel(a, b, c, out_a, out_b, out_c, hold_a, hold_b, hold_c, into, out_of):
    pieces = []
    rows = TOK // 4
    for n in range(4):
        span = pl.ds(n * rows, rows)
        pieces.append((a.at[span], hold_a.at[span], out_a.at[span]))
    pieces += [(b, hold_b, out_b), (c, hold_c, out_c)]
    starts = [pltpu.make_async_copy(p[0], p[1], into.at[i]) for i, p in enumerate(pieces)]
    ends = [pltpu.make_async_copy(p[1], p[2], out_of.at[i]) for i, p in enumerate(pieces)]
    for copy in starts:
        copy.start()
    for start, end in zip(starts, ends):
        start.wait()
        end.start()
    for copy in ends:
        copy.wait()


def emit(*results):
    hbm = pl.BlockSpec(memory_space=pltpu.HBM)
    results = [pltpu.with_memory_space_constraint(r, pltpu.HBM) for r in results]
    return pl.pallas_call(
        emit_kernel,
        out_shape=tuple(jax.ShapeDtypeStruct(r.shape, r.dtype) for r in results),
        in_specs=[hbm] * 3,
        out_specs=(hbm,) * 3,
        scratch_shapes=[pltpu.VMEM(r.shape, r.dtype) for r in results]
        + [pltpu.SemaphoreType.DMA((6,)), pltpu.SemaphoreType.DMA((6,))],
        name="emit",
    )(*results)


def local(queries, keys, values, grad_out, doc_lengths):
    return emit(*one_step(queries, grad_out, keys, values, doc_lengths))


def solution(mesh):
    split = P(("dp", "seq"), None)
    return jax.shard_map(
        local,
        mesh=mesh,
        in_specs=(split, split, split, split, P()),
        out_specs=(split, split, split),
        check_vma=False,
    )
```

profile of v0, /device:TPU:1, one launch (start us, length us, event | category | flops | bytes accessed | tf_op | source)
XLA Modules:
  0.0 79.7 jit_solution(3528393065282942777)
XLA Ops:
  0.6 77.0 %step.1 = (bf16[128,4096]{1,0:T(8,128)(2,1)}, bf16[128,512]{1,0:T(8,128)(2,1)}, bf16[128,512]{1,0:T(8,128)(2,1)}) custom-call(bf16[128,4096]{1,0:T(8,128)(2,1)} %q.1, bf16[128,4096]{1,0:T(8,128)(2,1)} %o.1, bf16[128,512]{1,0:T(8,128)(2,1)} %k.1, bf16[128,512]{1,0:T(8,128)(2,1)} %v.1, s32[32]{0:T(128)} %lens.1), custom_call_target="tpu_custom_call" | custom-call | tf_op jit(solution)/shard_map/step/pallas_call | solution.py:331
  77.6 2.1 %emit.1 = (bf16[128,4096]{1,0:T(8,128)(2,1)}, bf16[128,512]{1,0:T(8,128)(2,1)}, bf16[128,512]{1,0:T(8,128)(2,1)}) custom-call(bf16[128,4096]{1,0:T(8,128)(2,1)} %get-tuple-element.6.a, bf16[128,512]{1,0:T(8,128)(2,1)} %get-tuple-element.7.b, bf16[128,512]{1,0:T(8,128)(2,1)} %get-tuple-element.8.c), custom_call_target="tpu_custom_call" | custom-call | tf_op jit(solution)/shard_map/emit/pallas_call | solution.py:391
where the time goes:
time: 79.9 us; the launch traced here: 79.7 us
  Pallas kernels  79.1 us (99%)
    pallas_call x1, Pallas kernels, one_step(): pl.pallas_call(step_kernel, out_shape=(jax.ShapeDtypeStruct((TOK, SIDE *...  77 us
    pallas_call x1, Pallas kernels, emit(): pl.pallas_call(emit_kernel, out_shape=tuple((jax.ShapeDtypeStruct(r.shape...  2.1 us

commit v1 on v0

--- a/solution.py
+++ b/solution.py
@@ -17,6 +17,7 @@
 WIN = 2 * GROUP
 KB = 256
 SLOTS = 24
+BEHIND = 15
 EARLIEST = (0, 3, 8, 15)
 FROM_X = (0, 1, 3, 2)
 LOG2E = 1.4426950408889634
@@ -52,7 +53,7 @@
 def step_kernel(
     q, o, k, v, lens, out_q, out_k, out_v,
     land, kv, qs, os, s_buf, dp_buf, stats, run, final, dq, lows,
-    gq, z_out, z_in, own, y_out, y_in, x_out, send, recv, here,
+    terms, dqs, z_out, z_in, own, y_out, y_in, x_out, send, recv, here,
 ):
     dp, x, y = place()
     count = lax.axis_size("dp")
@@ -195,7 +196,9 @@
             tile = jnp.where(allowed, scores[:, span] * SCALE2, LOW)
             s_buf[i, :, :, span] = tile.reshape(2, TOK, HD)
             dprob = dprobs[:, span]
-            dp_buf[i, :, span] = dprob.astype(jnp.bfloat16)
+            dprob = dprob.astype(jnp.bfloat16)
+            dp_buf[i, :, span] = dprob
+            dprob = dprob.astype(jnp.float32)
             old = jnp.where(new_block, LOW, run[0, :, span])
             new = jnp.maximum(old, jnp.max(fold(tile), axis=0))
             weight = jnp.exp2(fold(tile) - new[None])
@@ -229,11 +232,30 @@
         final[slot, 0] = jnp.broadcast_to(peak + jnp.log2(total), part.shape)
         final[slot, 1] = jnp.broadcast_to(delta, part.shape)
 
+    behind = [
+        jnp.clip(lax.shift_right_arithmetic(17 - bases[slot], 1), 0, steps[slot])
+        for slot in range(SIDE)
+    ]
+    counts = behind + [steps[slot] - behind[slot] for slot in range(SIDE)]
+    opens = [jnp.int32(0)]
+    for n in range(2 * SIDE - 1):
+        opens.append(opens[-1] + counts[n])
+
+    def pick_run(run, values):
+        picked = values[0]
+        for n in range(1, 2 * SIDE):
+            picked = picked + at_least(run, n) * (values[n] - values[n - 1])
+        return picked
+
     dq[...] = jnp.zeros_like(dq)
 
-    @pl.loop(0, SLOTS)
-    def _(i):
-        slot, j, lead = step_of(i)
+    def grad_step(t):
+        part = sum(at_least(t, begin) for begin in opens[1:])
+        slot = part & 3
+        j = t - pick_run(part, opens)
+        at = jnp.minimum(j + at_least(part, SIDE) * pick(slot, behind), pick(slot, steps) - 1)
+        lead = jnp.minimum(pick(slot, bases) + 2 * at, WIN // TOK - 2)
+        i = jnp.clip(pick(slot, spots) + at, 0, SLOTS - 1)
         probs, dscores = [], []
         for h, span in enumerate(heads):
             prob = jnp.exp2(fold(s_buf[i, :, :, span]) - final[slot, 0, :, span][None])
@@ -243,82 +265,95 @@
             dscores.append(dscore.reshape(KB, TOK).astype(jnp.bfloat16))
         probs = jnp.concatenate(probs, axis=1)
         dscores = jnp.concatenate(dscores, axis=1)
-        s_buf[i, :, :, 0:HD] = dot(dscores, qs[slot], nn).reshape(2, TOK, HD)
-        s_buf[i, :, :, HD:2 * HD] = dot(probs, os[slot], nn).reshape(2, TOK, HD)
-        now = dq[...] * jnp.minimum(j, 1).astype(jnp.float32) + dot(rows(0, lead), dscores, tn)
+        terms[t, 1] = dot(probs, os[slot], nn).reshape(2, TOK, HD)
+        terms[t, 0] = dot(dscores, qs[slot], nn).reshape(2, TOK, HD)
+        now = dq[...] * jnp.clip(j, 0, 1).astype(jnp.float32) + dot(rows(0, lead), dscores, tn)
         dq[...] = now
-        dp_buf[i, 0:HD, :] = (now * INV_ROOT).astype(jnp.bfloat16)
+        dqs[t] = (now * INV_ROOT).astype(jnp.bfloat16)
 
     def key_sum(c):
         sums = [jnp.zeros((TOK, HD), jnp.float32)] * 2
         for slot in range(SIDE):
             off = c - bases[slot]
             inside = (at_least(off, 0) * at_least(2 * steps[slot] - 1, off)).astype(jnp.float32)
-            i = jnp.clip(spots[slot] + lax.shift_right_arithmetic(off, 1), 0, SLOTS - 1)
+            j = lax.shift_right_arithmetic(off, 1)
+            own_part = at_least(j, behind[slot])
+            t = j + opens[slot] + own_part * (opens[SIDE + slot] - opens[slot] - behind[slot])
+            t = jnp.clip(t, 0, SLOTS - 1)
             for n in range(2):
-                sums[n] += inside * s_buf[i, off & 1, :, n * HD:(n + 1) * HD]
+                sums[n] += inside * terms[t, n, off & 1]
         return sums[0] * INV_ROOT, sums[1]
 
+    order = (2, 1, 3, 0)
+    pl.loop(0, BEHIND)(grad_step)
     down = {}
-    order = (2, 1, 3, 0)
     for d in order:
-        column = lax.rem(y + d, SIDE)
+        row = lax.rem(x + d, SIDE)
 
         @pl.loop(0, SIDE)
-        def _(row):
+        def _(column):
             for n, total in enumerate(key_sum(row * SIDE + column)):
-                z_out[d, n, row] = total.astype(jnp.bfloat16)
+                z_out[d, n, column] = total.astype(jnp.bfloat16)
 
         down[d] = remote(z_out.at[d], z_in.at[d], before)
+    pl.loop(BEHIND, SLOTS)(grad_step)
 
     back_q = []
     for slot in (3, 1, 2, 0):
-        end = jnp.minimum(spots[slot] + steps[slot], SLOTS) - 1
+        ends = []
+        for n in (slot, SIDE + slot):
+            held = jnp.clip(opens[n] + counts[n] - 1, 0, SLOTS - 1)
+            ends.append((held, at_least(counts[n], 1).astype(jnp.float32)))
         for h, span in enumerate(heads):
-            gq[slot, :, span] = dp_buf[end, 0:HD, span].T
+            block = sum(weight * dqs[held, :, span].astype(jnp.float32) for held, weight in ends)
+            land[slot, 0, :, span] = block.T.astype(jnp.bfloat16)
         if slot:
-            back_q.append(remote(gq.at[slot], out_q.at[:, cols(x, GW)], at_x(FROM_X[slot])))
-    own_q = local_copy(gq.at[0], out_q.at[:, cols(x, GW)], 4)
-
-    across = {}
-    for d in order:
-        column = lax.rem(y + d, SIDE)
+            back_q.append(remote(land.at[slot, 0], out_q.at[:, cols(x, GW)], at_x(FROM_X[slot])))
+    own_q = local_copy(land.at[0, 0], out_q.at[:, cols(x, GW)], 4)
+
+    across, back = {}, []
+
+    def finish(d):
+        rest = own[order.index(d) % 2, :, y]
+        for e in (1, 2, 3):
+            across[d][e].wait_recv()
+            rest = rest + y_in[d, e - 1].astype(jnp.float32)
+        x_out[d] = rest.astype(jnp.bfloat16)
+        if d:
+            for n, out in enumerate((out_k, out_v)):
+                back.append(remote(x_out.at[d, n], out.at[:, cols(x, HD)], at_x(d)))
+
+    for n, d in enumerate(order):
+        row, side = lax.rem(x + d, SIDE), n % 2
 
         @pl.loop(0, SIDE)
-        def _(row):
+        def _(column):
             for n, total in enumerate(key_sum(GROUP // TOK + row * SIDE + column)):
-                own[d, n, row] = total
-
-    def total(d):
+                own[side, n, column] = total
+
         down[d].wait_recv()
-        return own[d] + z_in[d].astype(jnp.float32)
-
-    for d in order[:3]:
-        y_out[d - 1] = total(d).astype(jnp.bfloat16)
-        across[d] = remote(y_out.at[d - 1], y_in.at[d - 1], at_y(d))
-    rest = total(0)
-    for d in order[:3]:
-        across[d].wait_recv()
-        rest = rest + y_in[d - 1].astype(jnp.float32)
-    x_out[...] = rest.astype(jnp.bfloat16)
-    back = []
-    for d in (2, 1, 3):
-        target = lax.rem(x + d, SIDE)
-        for n, out in enumerate((out_k, out_v)):
-            back.append(remote(x_out.at[n, target], out.at[:, cols(x, HD)], at_x(d)))
-    own_kv = [local_copy(x_out.at[n, x], out.at[:, cols(x, HD)], 5 + n) for n, out in enumerate((out_k, out_v))]
+        own[side] = own[side] + z_in[d].astype(jnp.float32)
+        across[d] = {}
+        for e in (2, 1, 3):
+            y_out[d, e - 1] = own[side, :, lax.rem(y + e, SIDE)].astype(jnp.bfloat16)
+            across[d][e] = remote(y_out.at[d, e - 1], y_in.at[d, e - 1], at_y(e))
+        if n:
+            finish(order[n - 1])
+    finish(order[-1])
+    own_kv = [local_copy(x_out.at[0, n], out.at[:, cols(x, HD)], 5 + n) for n, out in enumerate((out_k, out_v))]
     for copy in back_q + back:
         copy.wait_recv()
     for copy in [own_q] + own_kv:
         copy.wait()
     gone = first + along + later + onward + back_q + back
-    for copies in list(arrive.values()) + [list(down.values()), list(across.values()), gone]:
+    gone += [copy for copies in across.values() for copy in copies.values()]
+    for copies in list(arrive.values()) + [list(down.values()), gone]:
         for copy in copies:
             copy.wait_send()
 
 
-VMEM_GRANT = 57 * 1024 * 1024
-COPIES = 6 + 6 + 2 + 2 + 4 + 4 + 3 + 3 + 6
+VMEM_GRANT = 67043328
+COPIES = 6 + 6 + 2 + 2 + 4 + 4 + 3 + 12 + 6
 
 
 def one_step(queries, grad_out, keys, values, doc_lengths):
@@ -349,13 +384,14 @@
             pltpu.VMEM((SIDE, 2, 8, wide), jnp.float32),
             pltpu.VMEM((HD, wide), jnp.float32),
             pltpu.VMEM((SIDE, 8, TOK), jnp.int32),
-            pltpu.VMEM((SIDE, TOK, GW), jnp.bfloat16),
+            pltpu.VMEM((SLOTS, 2, 2, TOK, HD), jnp.float32),
+            pltpu.VMEM((SLOTS, HD, wide), jnp.bfloat16),
             pltpu.VMEM((SIDE,) + piece, jnp.bfloat16),
             pltpu.VMEM((SIDE,) + piece, jnp.bfloat16),
-            pltpu.VMEM((SIDE,) + piece, jnp.float32),
-            pltpu.VMEM((3,) + piece, jnp.bfloat16),
-            pltpu.VMEM((3,) + piece, jnp.bfloat16),
-            pltpu.VMEM(piece, jnp.bfloat16),
+            pltpu.VMEM((2,) + piece, jnp.float32),
+            pltpu.VMEM((SIDE, 3, 2, TOK, HD), jnp.bfloat16),
+            pltpu.VMEM((SIDE, 3, 2, TOK, HD), jnp.bfloat16),
+            pltpu.VMEM((SIDE, 2, TOK, HD), jnp.bfloat16),
             pltpu.SemaphoreType.DMA((COPIES,)),
             pltpu.SemaphoreType.DMA((COPIES,)),
             pltpu.SemaphoreType.DMA((7,)),

time: 79.9 us -> 76.3 us (0.955)
  the two profiles are of different devices: /device:TPU:1 before, /device:TPU:64 now
where the time goes in v1:
time: 76.3 us; the launch traced here: 76.2 us
  Pallas kernels  75.5 us (99%)
    pallas_call x1, Pallas kernels, one_step(): pl.pallas_call(step_kernel, out_shape=(jax.ShapeDtypeStruct((TOK, SIDE *...  73.4 us
    pallas_call x1, Pallas kernels, emit(): pl.pallas_call(emit_kernel, out_shape=tuple((jax.ShapeDtypeStruct(r.shape...  2.1 us

profile of v1, /device:TPU:64, one launch (start us, length us, event | category | flops | bytes accessed | tf_op | source)
XLA Modules:
  0.0 76.2 jit_solution(6162938746643082076)
XLA Ops:
  0.6 73.4 %step.1 = (bf16[128,4096]{1,0:T(8,128)(2,1)}, bf16[128,512]{1,0:T(8,128)(2,1)}, bf16[128,512]{1,0:T(8,128)(2,1)}) custom-call(bf16[128,4096]{1,0:T(8,128)(2,1)} %q.1, bf16[128,4096]{1,0:T(8,128)(2,1)} %o.1, bf16[128,512]{1,0:T(8,128)(2,1)} %k.1, bf16[128,512]{1,0:T(8,128)(2,1)} %v.1, s32[32]{0:T(128)} %lens.1), custom_call_target="tpu_custom_call" | custom-call | tf_op jit(solution)/shard_map/step/pallas_call | solution.py:366
  74.1 2.1 %emit.1 = (bf16[128,4096]{1,0:T(8,128)(2,1)}, bf16[128,512]{1,0:T(8,128)(2,1)}, bf16[128,512]{1,0:T(8,128)(2,1)}) custom-call(bf16[128,4096]{1,0:T(8,128)(2,1)} %get-tuple-element.6.a, bf16[128,512]{1,0:T(8,128)(2,1)} %get-tuple-element.7.b, bf16[128,512]{1,0:T(8,128)(2,1)} %get-tuple-element.8.c), custom_call_target="tpu_custom_call" | custom-call | tf_op jit(solution)/shard_map/emit/pallas_call | solution.py:427

commit v2 on v1

--- a/solution.py
+++ b/solution.py
@@ -53,7 +53,7 @@
 def step_kernel(
     q, o, k, v, lens, out_q, out_k, out_v,
     land, kv, qs, os, s_buf, dp_buf, stats, run, final, dq, lows,
-    terms, dqs, z_out, z_in, own, y_out, y_in, x_out, send, recv, here,
+    terms, dqs, z_in, own, y_in, x_out, send, recv, here,
 ):
     dp, x, y = place()
     count = lax.axis_size("dp")
@@ -269,7 +269,7 @@
         terms[t, 0] = dot(dscores, qs[slot], nn).reshape(2, TOK, HD)
         now = dq[...] * jnp.clip(j, 0, 1).astype(jnp.float32) + dot(rows(0, lead), dscores, tn)
         dq[...] = now
-        dqs[t] = (now * INV_ROOT).astype(jnp.bfloat16)
+        dqs[t] = now.astype(jnp.bfloat16)
 
     def key_sum(c):
         sums = [jnp.zeros((TOK, HD), jnp.float32)] * 2
@@ -293,9 +293,15 @@
         @pl.loop(0, SIDE)
         def _(column):
             for n, total in enumerate(key_sum(row * SIDE + column)):
-                z_out[d, n, column] = total.astype(jnp.bfloat16)
-
-        down[d] = remote(z_out.at[d], z_in.at[d], before)
+                kv[n, 0, row, column] = total.astype(jnp.bfloat16)
+
+        if d:
+            down[d] = [remote(kv.at[:, 0, row], z_in.at[d], before)]
+        else:
+            down[d] = []
+            for e in order:
+                column = lax.rem(y + e, SIDE)
+                down[d].append(remote(kv.at[:, 0, row, column], z_in.at[d, :, column], before))
     pl.loop(BEHIND, SLOTS)(grad_step)
 
     back_q = []
@@ -303,7 +309,7 @@
         ends = []
         for n in (slot, SIDE + slot):
             held = jnp.clip(opens[n] + counts[n] - 1, 0, SLOTS - 1)
-            ends.append((held, at_least(counts[n], 1).astype(jnp.float32)))
+            ends.append((held, at_least(counts[n], 1).astype(jnp.float32) * INV_ROOT))
         for h, span in enumerate(heads):
             block = sum(weight * dqs[held, :, span].astype(jnp.float32) for held, weight in ends)
             land[slot, 0, :, span] = block.T.astype(jnp.bfloat16)
@@ -314,11 +320,13 @@
     across, back = {}, []
 
     def finish(d):
-        rest = own[order.index(d) % 2, :, y]
         for e in (1, 2, 3):
             across[d][e].wait_recv()
-            rest = rest + y_in[d, e - 1].astype(jnp.float32)
-        x_out[d] = rest.astype(jnp.bfloat16)
+        for n in range(2):
+            rest = own[order.index(d) % 2, n, y]
+            for e in (1, 2, 3):
+                rest = rest + y_in[d, e - 1, :, n * HD:(n + 1) * HD].astype(jnp.float32)
+            x_out[d, n] = rest.astype(jnp.bfloat16)
         if d:
             for n, out in enumerate((out_k, out_v)):
                 back.append(remote(x_out.at[d, n], out.at[:, cols(x, HD)], at_x(d)))
@@ -331,12 +339,18 @@
             for n, total in enumerate(key_sum(GROUP // TOK + row * SIDE + column)):
                 own[side, n, column] = total
 
-        down[d].wait_recv()
-        own[side] = own[side] + z_in[d].astype(jnp.float32)
         across[d] = {}
-        for e in (2, 1, 3):
-            y_out[d, e - 1] = own[side, :, lax.rem(y + e, SIDE)].astype(jnp.bfloat16)
-            across[d][e] = remote(y_out.at[d, e - 1], y_in.at[d, e - 1], at_y(e))
+        for e in order:
+            if d == 0 or e == order[0]:
+                down[d][order.index(e) if d == 0 else 0].wait_recv()
+            column = lax.rem(y + e, SIDE)
+            whole = own[side, :, column] + z_in[d, :, column].astype(jnp.float32)
+            if e:
+                leave = slice((e - 1) * 2 * HD, e * 2 * HD)
+                land[d, 1, :, leave] = jnp.concatenate([whole[0], whole[1]], axis=1).astype(jnp.bfloat16)
+                across[d][e] = remote(land.at[d, 1, :, leave], y_in.at[d, e - 1], at_y(e))
+            else:
+                own[side, :, column] = whole
         if n:
             finish(order[n - 1])
     finish(order[-1])
@@ -347,13 +361,13 @@
         copy.wait()
     gone = first + along + later + onward + back_q + back
     gone += [copy for copies in across.values() for copy in copies.values()]
-    for copies in list(arrive.values()) + [list(down.values()), gone]:
+    for copies in list(arrive.values()) + list(down.values()) + [gone]:
         for copy in copies:
             copy.wait_send()
 
 
-VMEM_GRANT = 67043328
-COPIES = 6 + 6 + 2 + 2 + 4 + 4 + 3 + 12 + 6
+VMEM_GRANT = 65536000
+COPIES = 6 + 6 + 2 + 2 + 4 + 7 + 3 + 12 + 6
 
 
 def one_step(queries, grad_out, keys, values, doc_lengths):
@@ -366,9 +380,9 @@
     return pl.pallas_call(
         step_kernel,
         out_shape=(
-            jax.ShapeDtypeStruct((TOK, SIDE * GW), jnp.bfloat16),
-            jax.ShapeDtypeStruct((TOK, SIDE * HD), jnp.bfloat16),
-            jax.ShapeDtypeStruct((TOK, SIDE * HD), jnp.bfloat16),
+            pltpu.VMEM((TOK, SIDE * GW), jnp.bfloat16),
+            pltpu.VMEM((TOK, SIDE * HD), jnp.bfloat16),
+            pltpu.VMEM((TOK, SIDE * HD), jnp.bfloat16),
         ),
         in_specs=[hbm] * 4 + [pl.BlockSpec(memory_space=pltpu.SMEM)],
         out_specs=(pl.BlockSpec(memory_space=pl.ANY),) * 3,
@@ -387,10 +401,8 @@
             pltpu.VMEM((SLOTS, 2, 2, TOK, HD), jnp.float32),
             pltpu.VMEM((SLOTS, HD, wide), jnp.bfloat16),
             pltpu.VMEM((SIDE,) + piece, jnp.bfloat16),
-            pltpu.VMEM((SIDE,) + piece, jnp.bfloat16),
             pltpu.VMEM((2,) + piece, jnp.float32),
-            pltpu.VMEM((SIDE, 3, 2, TOK, HD), jnp.bfloat16),
-            pltpu.VMEM((SIDE, 3, 2, TOK, HD), jnp.bfloat16),
+            pltpu.VMEM((SIDE, 3, TOK, 2 * HD), jnp.bfloat16),
             pltpu.VMEM((SIDE, 2, TOK, HD), jnp.bfloat16),
             pltpu.SemaphoreType.DMA((COPIES,)),
             pltpu.SemaphoreType.DMA((COPIES,)),
@@ -403,36 +415,27 @@
     )(*arguments, doc_lengths)
 
 
-def emit_kernel(a, b, c, out_a, out_b, out_c, hold_a, hold_b, hold_c, into, out_of):
-    pieces = []
-    rows = TOK // 4
-    for n in range(4):
-        span = pl.ds(n * rows, rows)
-        pieces.append((a.at[span], hold_a.at[span], out_a.at[span]))
-    pieces += [(b, hold_b, out_b), (c, hold_c, out_c)]
-    starts = [pltpu.make_async_copy(p[0], p[1], into.at[i]) for i, p in enumerate(pieces)]
-    ends = [pltpu.make_async_copy(p[1], p[2], out_of.at[i]) for i, p in enumerate(pieces)]
-    for copy in starts:
+def emit_kernel(a, b, c, out_a, out_b, out_c, sems):
+    copies = [
+        pltpu.make_async_copy(src, dst, sems.at[i])
+        for i, (src, dst) in enumerate(((a, out_a), (b, out_b), (c, out_c)))
+    ]
+    for copy in copies:
         copy.start()
-    for start, end in zip(starts, ends):
-        start.wait()
-        end.start()
-    for copy in ends:
+    for copy in copies:
         copy.wait()
 
 
 def emit(*results):
-    hbm = pl.BlockSpec(memory_space=pltpu.HBM)
-    results = [pltpu.with_memory_space_constraint(r, pltpu.HBM) for r in results]
     return pl.pallas_call(
         emit_kernel,
         out_shape=tuple(jax.ShapeDtypeStruct(r.shape, r.dtype) for r in results),
-        in_specs=[hbm] * 3,
-        out_specs=(hbm,) * 3,
-        scratch_shapes=[pltpu.VMEM(r.shape, r.dtype) for r in results]
-        + [pltpu.SemaphoreType.DMA((6,)), pltpu.SemaphoreType.DMA((6,))],
+        in_specs=[pl.BlockSpec(memory_space=pl.ANY)] * 3,
+        out_specs=(pl.BlockSpec(memory_space=pltpu.HBM),) * 3,
+        scratch_shapes=[pltpu.SemaphoreType.DMA((3,))],
+        compiler_params=pltpu.CompilerParams(vmem_limit_bytes=1024 * 1024),
         name="emit",
-    )(*results)
+    )(*(pltpu.with_memory_space_constraint(r, pltpu.VMEM) for r in results))
 
 
 def local(queries, keys, values, grad_out, doc_lengths):

time: 76.3 us -> 74.9 us (0.982)
  Pallas kernels: 75.5 us -> 73.7 us
    pallas_call x1, Pallas kernels: 2.1 us -> 1.07 us  [emit(): pl.pallas_call(emit_kernel, out_shape=tuple((jax.ShapeDtypeStruct(r.shape...]
    pallas_call x1, Pallas kernels: 73.4 us -> 72.6 us  [one_step(): pl.pallas_call(step_kernel, out_shape=(pltpu.VMEM((TOK, SIDE * GW), jnp.b...]
where the time goes in v2:
time: 74.9 us; the launch traced here: 74.3 us
  Pallas kernels  73.7 us (98%)
    pallas_call x1, Pallas kernels, one_step(): pl.pallas_call(step_kernel, out_shape=(pltpu.VMEM((TOK, SIDE * GW), jnp.b...  72.6 us

profile of v2, /device:TPU:64, one launch (start us, length us, event | category | flops | bytes accessed | tf_op | source)
XLA Modules:
  0.0 74.3 jit_solution(15163653687316421298)
XLA Ops:
  0.6 72.6 %step.1 = (bf16[128,4096]{1,0:T(8,128)(2,1)S(1)}, bf16[128,512]{1,0:T(8,128)(2,1)S(1)}, bf16[128,512]{1,0:T(8,128)(2,1)S(1)}) custom-call(bf16[128,4096]{1,0:T(8,128)(2,1)} %q.1, bf16[128,4096]{1,0:T(8,128)(2,1)} %o.1, bf16[128,512]{1,0:T(8,128)(2,1)} %k.1, bf16[128,512]{1,0:T(8,128)(2,1)} %v.1, s32[32]{0:T(128)} %lens.1), custom_call_target="tpu_custom_call" | custom-call | tf_op jit(solution)/shard_map/step/pallas_call | solution.py:380
  73.2 1.1 %emit.1 = (bf16[128,4096]{1,0:T(8,128)(2,1)}, bf16[128,512]{1,0:T(8,128)(2,1)}, bf16[128,512]{1,0:T(8,128)(2,1)}) custom-call(bf16[128,4096]{1,0:T(8,128)(2,1)S(1)} %get-tuple-element.6.a, bf16[128,512]{1,0:T(8,128)(2,1)S(1)} %get-tuple-element.7.b, bf16[128,512]{1,0:T(8,128)(2,1)S(1)} %get-tuple-element.8.c), custom_call_target="tpu_custom_call" | custom-call | tf_op jit(solution)/shard_map/emit/pallas_call | solution.py:430

commit v3 on v2

--- a/solution.py
+++ b/solution.py
@@ -287,7 +287,8 @@
     order = (2, 1, 3, 0)
     pl.loop(0, BEHIND)(grad_step)
     down = {}
-    for d in order:
+
+    def send_row(d):
         row = lax.rem(x + d, SIDE)
 
         @pl.loop(0, SIDE)
@@ -302,10 +303,15 @@
             for e in order:
                 column = lax.rem(y + e, SIDE)
                 down[d].append(remote(kv.at[:, 0, row, column], z_in.at[d, :, column], before))
+    for d in order[:2]:
+        send_row(d)
     pl.loop(BEHIND, SLOTS)(grad_step)
 
     back_q = []
     for slot in (3, 1, 2, 0):
+        if slot == 0:
+            for d in order[2:]:
+                send_row(d)
         ends = []
         for n in (slot, SIDE + slot):
             held = jnp.clip(opens[n] + counts[n] - 1, 0, SLOTS - 1)

time: 74.9 us -> 75.3 us (level)
  no operation moved by 1% of the time
where the time goes in v3:
time: 75.3 us; the launch traced here: 74.3 us
  Pallas kernels  73.7 us (98%)
    pallas_call x1, Pallas kernels, one_step(): pl.pallas_call(step_kernel, out_shape=(pltpu.VMEM((TOK, SIDE * GW), jnp.b...  72.6 us

profile of v3, /device:TPU:64, one launch (start us, length us, event | category | flops | bytes accessed | tf_op | source)
XLA Modules:
  0.0 74.3 jit_solution(7637284645194587320)
XLA Ops:
  0.6 72.6 %step.1 = (bf16[128,4096]{1,0:T(8,128)(2,1)S(1)}, bf16[128,512]{1,0:T(8,128)(2,1)S(1)}, bf16[128,512]{1,0:T(8,128)(2,1)S(1)}) custom-call(bf16[128,4096]{1,0:T(8,128)(2,1)} %q.1, bf16[128,4096]{1,0:T(8,128)(2,1)} %o.1, bf16[128,512]{1,0:T(8,128)(2,1)} %k.1, bf16[128,512]{1,0:T(8,128)(2,1)} %v.1, s32[32]{0:T(128)} %lens.1), custom_call_target="tpu_custom_call" | custom-call | tf_op jit(solution)/shard_map/step/pallas_call | solution.py:386
  73.3 1.1 %emit.1 = (bf16[128,4096]{1,0:T(8,128)(2,1)}, bf16[128,512]{1,0:T(8,128)(2,1)}, bf16[128,512]{1,0:T(8,128)(2,1)}) custom-call(bf16[128,4096]{1,0:T(8,128)(2,1)S(1)} %get-tuple-element.6.a, bf16[128,512]{1,0:T(8,128)(2,1)S(1)} %get-tuple-element.7.b, bf16[128,512]{1,0:T(8,128)(2,1)S(1)} %get-tuple-element.8.c), custom_call_target="tpu_custom_call" | custom-call | tf_op jit(solution)/shard_map/emit/pallas_call | solution.py:436

commit v4 on v2

--- a/solution.py
+++ b/solution.py
@@ -269,7 +269,7 @@
         terms[t, 0] = dot(dscores, qs[slot], nn).reshape(2, TOK, HD)
         now = dq[...] * jnp.clip(j, 0, 1).astype(jnp.float32) + dot(rows(0, lead), dscores, tn)
         dq[...] = now
-        dqs[t] = now.astype(jnp.bfloat16)
+        dqs[t] = (now * INV_ROOT).astype(jnp.bfloat16)
 
     def key_sum(c):
         sums = [jnp.zeros((TOK, HD), jnp.float32)] * 2
@@ -309,7 +309,7 @@
         ends = []
         for n in (slot, SIDE + slot):
             held = jnp.clip(opens[n] + counts[n] - 1, 0, SLOTS - 1)
-            ends.append((held, at_least(counts[n], 1).astype(jnp.float32) * INV_ROOT))
+            ends.append((held, at_least(counts[n], 1).astype(jnp.float32)))
         for h, span in enumerate(heads):
             block = sum(weight * dqs[held, :, span].astype(jnp.float32) for held, weight in ends)
             land[slot, 0, :, span] = block.T.astype(jnp.bfloat16)

time: 74.9 us -> 75 us (level)
  no operation moved by 1% of the time
where the time goes in v4:
time: 75 us; the launch traced here: 74.3 us
  Pallas kernels  73.7 us (98%)
    pallas_call x1, Pallas kernels, one_step(): pl.pallas_call(step_kernel, out_shape=(pltpu.VMEM((TOK, SIDE * GW), jnp.b...  72.6 us

profile of v4, /device:TPU:64, one launch (start us, length us, event | category | flops | bytes accessed | tf_op | source)
XLA Modules:
  0.0 74.3 jit_solution(11293938088544110798)
XLA Ops:
  0.6 72.6 %step.1 = (bf16[128,4096]{1,0:T(8,128)(2,1)S(1)}, bf16[128,512]{1,0:T(8,128)(2,1)S(1)}, bf16[128,512]{1,0:T(8,128)(2,1)S(1)}) custom-call(bf16[128,4096]{1,0:T(8,128)(2,1)} %q.1, bf16[128,4096]{1,0:T(8,128)(2,1)} %o.1, bf16[128,512]{1,0:T(8,128)(2,1)} %k.1, bf16[128,512]{1,0:T(8,128)(2,1)} %v.1, s32[32]{0:T(128)} %lens.1), custom_call_target="tpu_custom_call" | custom-call | tf_op jit(solution)/shard_map/step/pallas_call | solution.py:380
  73.2 1.1 %emit.1 = (bf16[128,4096]{1,0:T(8,128)(2,1)}, bf16[128,512]{1,0:T(8,128)(2,1)}, bf16[128,512]{1,0:T(8,128)(2,1)}) custom-call(bf16[128,4096]{1,0:T(8,128)(2,1)S(1)} %get-tuple-element.6.a, bf16[128,512]{1,0:T(8,128)(2,1)S(1)} %get-tuple-element.7.b, bf16[128,512]{1,0:T(8,128)(2,1)S(1)} %get-tuple-element.8.c), custom_call_target="tpu_custom_call" | custom-call | tf_op jit(solution)/shard_map/emit/pallas_call | solution.py:430
